TPU v7x, 128 devices: a whole 4x4x4 slice. The times are simulated.
128 devices in a mesh: expert: 16 (over z, y), tensor: 8 (over x, core).
Axes of the slice: x: 4, y: 4, z: 4, core: 2. Of those that a mesh axis runs over, the one named last changes fastest.
Arguments:
- layer_input: bfloat16 [4096, 2, 4096], P('expert', None, 'tensor'), may hold values from -6 to 6
- base_input: bfloat16 [4096, 4096], P('expert', 'tensor'), may hold values from -6 to 6
- cotangent: bfloat16 [4096, 4096], P('expert', 'tensor'), may hold values from -6 to 6
- cross_weight: bfloat16 [16, 2, 4096, 4096], P('expert', None, 'tensor'), may hold values from -0.0625 to 0.0625
- cross_bias: float32 [16, 4096], P('expert', 'tensor'), may hold values from -3 to 3
- routes: int32 [4096, 2], P('expert'), may hold values from 0 to 15, as said below
- gate_values: float32 [4096, 2], P('expert'), may hold values from 0.2 to 1
Outputs:
- layer_out: bfloat16 [4096, 4096], P('expert', 'tensor')
- input_grad: bfloat16 [4096, 2, 4096], P('expert', None, 'tensor')
- base_grad: bfloat16 [4096, 4096], P('expert', 'tensor')
- weight_grad: bfloat16 [16, 2, 4096, 4096], P('expert', None, 'tensor')
- bias_grad: float32 [16, 4096], P('expert', 'tensor')
Inputs may be any that keep to these rules, and one draw needn't show every extreme that they name: `routes`: each row names two different experts. Among the 256 rows of one index of expert (aligned blocks), no expert is named more than 48 times, and one expert, the same in every block, is named exactly 48 times in every block.
All inputs are finite; a program needn't handle non-finite values.
Results may differ from a plain program's by a relative error of at most 0.017.
Values may be sent and summed in bfloat16 or wider, within the bound.
A program may use at most 128 MiB of HBM per device.

v0:
```python
import jax
import jax.numpy as jnp
from jax import lax
from jax.sharding import PartitionSpec as P


def route_positions(routes, experts, capacity):
    flat_routes = routes.reshape(-1)
    one_hot = (flat_routes[:, None] == jnp.arange(experts, dtype=jnp.int32)[None, :]).astype(
        jnp.int32
    )
    ranks = jnp.cumsum(one_hot, axis=0) - one_hot
    return flat_routes * capacity + jnp.sum(ranks * one_hot, axis=1)


def per_device(layer_input, base_input, cotangent, cross_weight, cross_bias, routes, gate_values):
    rows = layer_input.shape[0]
    width = layer_input.shape[2]
    full_out = cross_weight.shape[3]
    experts = lax.axis_size("expert")
    capacity = (3 * rows + experts - 1) // experts
    slots_total = experts * capacity
    scale = 1.0 / jnp.sqrt(jnp.float32(2 * rows))
    positions = route_positions(routes, experts, capacity)
    route_inputs = jnp.broadcast_to(layer_input[:, None], (rows, 2, 2, width)).reshape(
        2 * rows, 2, width
    )
    send_inputs = jnp.zeros((slots_total, 2, width), jnp.bfloat16).at[positions].set(route_inputs)
    send_inputs = send_inputs.reshape(experts, capacity, 2, width)
    weighted = (cotangent.astype(jnp.float32) * base_input.astype(jnp.float32)).astype(jnp.bfloat16)
    weighted_rows = lax.all_gather(weighted, "tensor", axis=1, tiled=True)
    cot_width = weighted_rows.shape[1]
    route_cot = (gate_values[:, :, None] * weighted_rows[:, None, :].astype(jnp.float32)).astype(
        jnp.bfloat16
    )
    send_cot = (
        jnp.zeros((slots_total, cot_width), jnp.bfloat16)
        .at[positions]
        .set(route_cot.reshape(2 * rows, cot_width))
    )
    send_cot = send_cot.reshape(experts, capacity, cot_width)
    arrived_inputs, arrived_cot = (
        lax.all_to_all(send_inputs, "expert", split_axis=0, concat_axis=0, tiled=True),
        lax.all_to_all(send_cot, "expert", split_axis=0, concat_axis=0, tiled=True),
    )
    flat_inputs = arrived_inputs.reshape(slots_total, 2 * width)
    flat_weight = cross_weight.reshape(2 * width, full_out)
    partial_value = jnp.dot(flat_inputs, flat_weight, preferred_element_type=jnp.float32)
    summed = lax.psum_scatter(
        partial_value.astype(jnp.bfloat16), "tensor", scatter_dimension=1, tiled=True
    ).astype(jnp.float32)
    cross = (summed + cross_bias).astype(jnp.bfloat16)
    returned = lax.all_to_all(
        cross.reshape(experts, capacity, width), "expert", split_axis=0, concat_axis=0, tiled=True
    )
    cross_routes = (
        returned.reshape(slots_total, width)[positions].reshape(rows, 2, width).astype(jnp.float32)
    )
    mixture = jnp.sum(gate_values[:, :, None] * cross_routes, axis=1)
    gate_total = jnp.sum(gate_values, axis=1)[:, None]
    layer_out = (
        base_input.astype(jnp.float32) * mixture
        + gate_total * layer_input[:, 0, :].astype(jnp.float32)
    ).astype(jnp.bfloat16)
    base_grad = (cotangent.astype(jnp.float32) * mixture).astype(jnp.bfloat16)
    cot_rows = arrived_cot.reshape(slots_total, cot_width)
    weight_sum = lax.dot_general(
        flat_inputs, cot_rows, (((0,), (0,)), ((), ())), preferred_element_type=jnp.float32
    )
    route_grads = lax.dot_general(
        cot_rows, flat_weight, (((1,), (1,)), ((), ())), preferred_element_type=jnp.float32
    )
    own_columns = lax.dynamic_slice_in_dim(cot_rows, lax.axis_index("tensor") * width, width, 1)
    bias_sum = jnp.sum(own_columns.astype(jnp.float32), axis=0)
    weight_grad = (weight_sum * scale).astype(jnp.bfloat16).reshape(1, 2, width, full_out)
    bias_grad = (bias_sum * scale).reshape(1, width)
    route_back = lax.all_to_all(
        route_grads.astype(jnp.bfloat16).reshape(experts, capacity, 2, width),
        "expert",
        split_axis=0,
        concat_axis=0,
        tiled=True,
    )
    picked = (
        route_back.reshape(slots_total, 2, width)[positions]
        .reshape(rows, 2, 2, width)
        .astype(jnp.float32)
    )
    grad_sum = jnp.sum(picked, axis=1)
    grad_sum = grad_sum.at[:, 0, :].add(gate_total * cotangent.astype(jnp.float32))
    input_grad = grad_sum.astype(jnp.bfloat16)
    return (layer_out, input_grad, base_grad, weight_grad, bias_grad)


def solution(mesh):
    in_specs = (
        P("expert", None, "tensor"),
        P("expert", "tensor"),
        P("expert", "tensor"),
        P("expert", None, "tensor", None),
        P("expert", "tensor"),
        P("expert", None),
        P("expert", None),
    )
    out_specs = (
        P("expert", "tensor"),
        P("expert", None, "tensor"),
        P("expert", "tensor"),
        P("expert", None, "tensor", None),
        P("expert", "tensor"),
    )
    return jax.shard_map(
        per_device, mesh=mesh, in_specs=in_specs, out_specs=out_specs, check_vma=False
    )
```

profile of v0, /device:TPU:0, one launch (start us, length us, event | category | flops | bytes accessed | tf_op | source)
XLA Modules:
  0.0 356.7 jit_solution(16559496350380601480)
XLA Ops:
  7.2 0.0 reduce-scatter.2.cloned.1.call-start
  7.2 0.7 broadcast_multiply_fusion.1
  7.9 0.8 copy.32
  8.7 0.1 eq.29
  8.9 0.1 eq.25
  9.0 0.1 copy.31
  9.1 0.1 mul.96
  9.3 1.2 reduce-window.6
  10.5 0.2 slice_reduce_fusion
  10.7 0.1 fusion.9
  10.8 1.6 broadcast_in_dim.7
  12.4 0.8 broadcast_in_dim.6
  13.2 13.8 %scatter_fusion = bf16[768,2,512]{2,1,0:T(2,128)(2,1)S(1)} fusion(bf16[768,2,512]{2,1,0:T(2,128)(2,1)S(1)} %broadcast_in_dim.6, s32[512]{0:T(512)S(1)} %bitcast.61, bf16[512,2,512]{2,1,0:T(2,128)(2,1)S(1)} %bitcast.57), kind=kCustom, calls=%fused_computation.2 | custom fusion | bytes 3147776 | tf_op jit(solution)/shard_map/scatter | solution.py:28
  27.1 30.7 %all_to_all.20 = bf16[16,48,2,512]{3,2,1,0:T(2,128)(2,1)S(1)} all-to-all(bf16[16,48,2,512]{3,2,1,0:T(2,128)(2,1)S(1)} %bitcast.54), channel_id=1, replica_groups=mesh['expert'=16,'tensor'=8] {'expert'}, dimensions={0} | all-to-all | bytes 3145728 | tf_op jit(solution)/shard_map/all_to_all | solution.py:43
  57.8 0.4 copy.39
  58.2 0.0 copy-start.1
  58.2 1.2 copy-done.1
  59.5 11.9 %convolution_convert_fusion = bf16[768,4096]{1,0:T(8,128)(2,1)} fusion(bf16[768,1024]{1,0:T(8,128)(2,1)S(1)} %bitcast.59, bf16[1024,4096]{1,0:T(8,128)(2,1)} %bitcast.67), kind=kOutput, calls=%fused_computation.6 | convolution fusion | flops 6445596672 | bytes 16252928 | tf_op jit(solution)/shard_map/dot_general | solution.py:48
  71.4 0.0 copy-start.5
  71.4 0.0 copy-start.4
  71.4 0.0 reduce-scatter.2.cloned.1.call-update
  71.4 0.0 copy-start
  71.4 0.0 copy-start.2
  71.4 0.0 copy-start.3
  71.4 40.0 %reduce-scatter.2.cloned.1.call-done = bf16[768,512]{1,0:T(8,128)(2,1)} async-done(((bf16[768,4096]{1,0:T(8,128)(2,1)}), bf16[768,512]{1,0:T(8,128)(2,1)}) %reduce-scatter.2.cloned.1.call-update) | async-done | bytes 786448 | tf_op jit(solution)/shard_map/reduce_scatter | solution.py:49
  111.5 0.0 copy-done.5
  111.5 2.2 add_convert_fusion
  113.6 7.0 %all-to-all-start.1 = ((bf16[16,48,512]{2,1,0:T(8,128)(2,1)}), bf16[16,48,512]{2,1,0:T(8,128)(2,1)S(1)}, u32[]{:S(2)}, u32[]{:S(2)}) async-start(bf16[16,48,512]{2,1,0:T(8,128)(2,1)} %bitcast.7), calls=%async_computation.2 | async-start | bytes 1572864 | tf_op jit(solution)/shard_map/all_to_all | solution.py:53
  120.6 0.2 all-gather.2.cloned.1.call-start
  120.8 0.0 copy-done.4
  120.9 0.1 copy.30
  121.0 13.4 %all-to-all-done.1 = bf16[16,48,512]{2,1,0:T(8,128)(2,1)S(1)} async-done(((bf16[16,48,512]{2,1,0:T(8,128)(2,1)}), bf16[16,48,512]{2,1,0:T(8,128)(2,1)S(1)}, u32[]{:S(2)}, u32[]{:S(2)}) %all-to-all-start.1) | async-done | bytes 786464 | tf_op jit(solution)/shard_map/all_to_all | solution.py:53
  134.4 2.0 gather_fusion
  136.4 0.7 reshape.161
  137.1 1.3 multiply_reduce_fusion
  138.4 0.0 copy-done
  138.4 0.0 copy-done.2
  138.4 0.0 copy-done.3
  138.4 1.1 fusion.6
  139.5 0.0 all-gather.2.cloned.1.call-update
  139.5 0.1 mul.102
  139.7 22.7 %all-gather.2.cloned.1.call-done = bf16[256,4096]{1,0:T(8,128)(2,1)} async-done(((bf16[256,512]{1,0:T(8,128)(2,1)}), bf16[256,4096]{1,0:T(8,128)(2,1)}) %all-gather.2.cloned.1.call-update) | async-done | bytes 2097168 | tf_op jit(solution)/shard_map/all_gather | solution.py:31
  162.4 8.2 %mul.105 = f32[256,2,4096]{2,1,0:T(2,128)} broadcast(bf16[256,4096]{1,0:T(8,128)(2,1)} %all-gather.2.cloned.1.call-done), dimensions={0,2} | broadcast | bytes 10485760 | tf_op jit(solution)/shard_map/mul | solution.py:33
  170.6 10.9 %mul.106 = f32[512,4096]{1,0:T(8,128)} reshape(f32[256,2,4096]{2,1,0:T(2,128)} %mul.105) | data formatting | bytes 16777216 | tf_op jit(solution)/shard_map/mul | solution.py:33
  181.5 12.7 %scatter_custom_fusion.1 = bf16[768,4096]{1,0:T(8,128)(2,1)} fusion(s32[512]{0:T(512)S(1)} %bitcast.63, f32[512,4096]{1,0:T(8,128)} %mul.106, f32[512]{0:T(512)S(1)} %mul.102, bf16[]{:T(256)} %constant.44.clone.1), kind=kCustom, calls=%fused_computation.7 | custom fusion | flops 4194304 | bytes 14682114 | tf_op jit(solution)/shard_map/scatter | solution.py:39
  194.2 7.0 %all-to-all-start.2 = ((bf16[16,48,4096]{2,1,0:T(8,128)(2,1)}), bf16[16,48,4096]{2,1,0:T(8,128)(2,1)}, u32[]{:S(2)}, u32[]{:S(2)}) async-start(bf16[16,48,4096]{2,1,0:T(8,128)(2,1)} %bitcast.53), calls=%async_computation.3 | async-start | bytes 12582912 | tf_op jit(solution)/shard_map/all_to_all | solution.py:44
  201.2 94.4 %all-to-all-done.2 = bf16[16,48,4096]{2,1,0:T(8,128)(2,1)} async-done(((bf16[16,48,4096]{2,1,0:T(8,128)(2,1)}), bf16[16,48,4096]{2,1,0:T(8,128)(2,1)}, u32[]{:S(2)}, u32[]{:S(2)}) %all-to-all-start.2) | async-done | bytes 6291488 | tf_op jit(solution)/shard_map/all_to_all | solution.py:44
  295.7 11.0 %convolution_convert_fusion.1 = bf16[768,1024]{1,0:T(8,128)(2,1)S(1)} fusion(bf16[768,4096]{1,0:T(8,128)(2,1)} %bitcast.11, bf16[1024,4096]{1,0:T(8,128)(2,1)} %bitcast.68), kind=kOutput, calls=%fused_computation.11 | convolution fusion | flops 6443237376 | bytes 16252928 | tf_op jit(solution)/shard_map/dot_general | solution.py:70
  306.6 1.3 convert_reduce_fusion.1
  307.9 2.4 reshape.157
  310.3 5.0 %all-to-all-start.3 = ((bf16[16,48,2,512]{3,2,1,0:T(2,128)(2,1)}), bf16[16,48,2,512]{3,2,1,0:T(2,128)(2,1)S(1)}, u32[]{:S(2)}, u32[]{:S(2)}) async-start(bf16[16,48,2,512]{3,2,1,0:T(2,128)(2,1)} %reshape.157), calls=%async_computation.4 | async-start | bytes 3145728 | tf_op jit(solution)/shard_map/all_to_all | solution.py:77
  315.3 0.6 broadcast_multiply_fusion
  315.9 11.4 %multiply_convert_fusion = bf16[1024,4096]{1,0:T(8,128)(2,1)} fusion(bf16[768,1024]{1,0:T(8,128)(2,1)} %bitcast.60, bf16[768,4096]{1,0:T(8,128)(2,1)} %bitcast.11), kind=kOutput, calls=%fused_computation.4 | convolution fusion | flops 6450839552 | bytes 16252928 | tf_op jit(solution)/shard_map/dot_general | solution.py:67
  327.2 11.3 %all-to-all-done.3 = bf16[16,48,2,512]{3,2,1,0:T(2,128)(2,1)S(1)} async-done(((bf16[16,48,2,512]{3,2,1,0:T(2,128)(2,1)}), bf16[16,48,2,512]{3,2,1,0:T(2,128)(2,1)S(1)}, u32[]{:S(2)}, u32[]{:S(2)}) %all-to-all-start.3) | async-done | bytes 1572896 | tf_op jit(solution)/shard_map/all_to_all | solution.py:77
  338.5 3.6 gather_fusion.1
  342.1 1.4 convert_reduce_fusion
  343.5 0.5 slice_add_fusion
  344.0 4.7 %scatter-add.4 = f32[256,2,512]{2,1,0:T(2,128)S(1)} dynamic-update-slice(f32[256,2,512]{2,1,0:T(2,128)S(1)} %convert_reduce_fusion, f32[256,1,512]{2,1,0:T(1,128)S(1)} %slice_add_fusion, s32[]{:T(128)} %constant.46.clone.1, s32[]{:T(128)} %constant.46.clone.1, s32[]{:T(128)} %constant.46.clone.1) | dynamic-update-slice | bytes 1048580 | tf_op jit(solution)/shard_map/scatter-add | solution.py:90
  348.8 1.2 convert_element_type.90
  (6 shorter events, 0.1 us)
Async XLA Ops:
  7.2 104.3 %reduce-scatter.2.cloned.1.call-start = ((), (), s32[]{:S(2)}) async-start(), calls=%async_computation.5 | async-start | bytes 7077888 | tf_op jit(solution)/shard_map/reduce_scatter | solution.py:49
  58.2 1.2 copy-start.1
  71.4 40.1 %copy-start.5 = (f32[1,512]{1,0:T(1,128)S(1)}, f32[1,512]{1,0:T(1,128)}, u32[]{:S(2)}) copy-start(f32[1,512]{1,0:T(1,128)} %param.13) | copy-start | bytes 6148
  71.4 49.5 %copy-start.4 = (f32[256,2]{0,1:T(2,128)S(1)}, f32[256,2]{0,1:T(2,128)}, u32[]{:S(2)}) copy-start(f32[256,2]{0,1:T(2,128)} %param.15) | copy-start | bytes 6148
  71.4 67.0 %copy-start = (bf16[256,2,512]{2,1,0:T(2,128)(2,1)S(1)}, bf16[256,2,512]{2,1,0:T(2,128)(2,1)}, u32[]{:S(2)}) copy-start(bf16[256,2,512]{2,1,0:T(2,128)(2,1)} %param.9) | copy-start | bytes 1572868
  71.4 67.0 %copy-start.2 = (bf16[256,512]{1,0:T(8,128)(2,1)S(1)}, bf16[256,512]{1,0:T(8,128)(2,1)}, u32[]{:S(2)}) copy-start(bf16[256,512]{1,0:T(8,128)(2,1)} %param.11) | copy-start | bytes 786436
  71.4 67.0 %copy-start.3 = (bf16[256,512]{1,0:T(8,128)(2,1)S(1)}, bf16[256,512]{1,0:T(8,128)(2,1)}, u32[]{:S(2)}) copy-start(bf16[256,512]{1,0:T(8,128)(2,1)} %param.10) | copy-start | bytes 786436
  113.6 20.8 %all-to-all-start.1 = ((bf16[16,48,512]{2,1,0:T(8,128)(2,1)}), bf16[16,48,512]{2,1,0:T(8,128)(2,1)S(1)}, u32[]{:S(2)}, u32[]{:S(2)}) async-start(bf16[16,48,512]{2,1,0:T(8,128)(2,1)} %bitcast.7), calls=%async_computation.2 | async-start | bytes 1572864 | tf_op jit(solution)/shard_map/all_to_all | solution.py:53
  120.6 41.8 %all-gather.2.cloned.1.call-start = ((), (), s32[]{:S(2)}) async-start(), calls=%async_computation.6 | async-start | bytes 2359296 | tf_op jit(solution)/shard_map/all_gather | solution.py:31
  194.2 101.5 %all-to-all-start.2 = ((bf16[16,48,4096]{2,1,0:T(8,128)(2,1)}), bf16[16,48,4096]{2,1,0:T(8,128)(2,1)}, u32[]{:S(2)}, u32[]{:S(2)}) async-start(bf16[16,48,4096]{2,1,0:T(8,128)(2,1)} %bitcast.53), calls=%async_computation.3 | async-start | bytes 12582912 | tf_op jit(solution)/shard_map/all_to_all | solution.py:44
  310.3 28.2 %all-to-all-start.3 = ((bf16[16,48,2,512]{3,2,1,0:T(2,128)(2,1)}), bf16[16,48,2,512]{3,2,1,0:T(2,128)(2,1)S(1)}, u32[]{:S(2)}, u32[]{:S(2)}) async-start(bf16[16,48,2,512]{3,2,1,0:T(2,128)(2,1)} %reshape.157), calls=%async_computation.4 | async-start | bytes 3145728 | tf_op jit(solution)/shard_map/all_to_all | solution.py:77
Sparse Core Ops, SparseCore 0:
  71.5 39.9 reduce-scatter.1
  139.6 22.7 all-gather.1
where the time goes:
time: 358 us; the launch traced here: 357 us
  waiting for transfers between devices  182 us (51%)
  local copies, waits for them, and re-layouts  52 us (15%)
  matrix products  34.2 us (10%)
  blocking collectives  30.7 us (9%)
  other arithmetic  24.3 us (7%)
  starting transfers between devices  19.2 us (5%)
  between operations  14.3 us (4%)
    all_to_all x1, waiting for transfers between devices, per_device(): lax.all_to_all(send_cot, 'expert', split_axis=0, concat_axis=0, tiled=True)  94.4 us
    reduce_scatter x1, waiting for transfers between devices, per_device(): lax.psum_scatter(partial_value.astype(jnp.bfloat16), 'tensor', scatter_di...  40 us
    all_to_all x1, blocking collectives, per_device(): lax.all_to_all(send_inputs, 'expert', split_axis=0, concat_axis=0, tiled=...  30.7 us
    all_gather x1, waiting for transfers between devices, per_device(): weighted_rows = lax.all_gather(weighted, 'tensor', axis=1, tiled=True)  22.7 us
    mul x3, local copies, waits for them, and re-layouts, per_device(): gate_values[:, :, None] * weighted_rows[:, None, :].astype(jnp.float32)  19.2 us
    scatter x1, local copies, waits for them, and re-layouts, per_device(): jnp.zeros((slots_total, 2, width), jnp.bfloat16).at[positions]  13.8 us
    all_to_all x1, waiting for transfers between devices, per_device(): lax.all_to_all(cross.reshape(experts, capacity, width), 'expert', split_a...  13.4 us
    scatter x1, other arithmetic, per_device(): send_cot = jnp.zeros((slots_total, cot_width), jnp.bfloat16).at[positions...  12.7 us
  transfers between devices with their start and end apart: 5, of which 5 were waited for; matrix products, arithmetic and copies ran while one was open for 3% of the time, Pallas kernels for 0%

commit v1 on v0

--- a/solution.py
+++ b/solution.py
@@ -28,7 +28,18 @@
     send_inputs = jnp.zeros((slots_total, 2, width), jnp.bfloat16).at[positions].set(route_inputs)
     send_inputs = send_inputs.reshape(experts, capacity, 2, width)
     weighted = (cotangent.astype(jnp.float32) * base_input.astype(jnp.float32)).astype(jnp.bfloat16)
-    weighted_rows = lax.all_gather(weighted, "tensor", axis=1, tiled=True)
+    ways = lax.axis_size("tensor")
+    up = [(d, (d + 1) % ways) for d in range(ways)]
+    down = [(d, (d - 1) % ways) for d in range(ways)]
+    earlier, later = ([weighted], [weighted])
+    for _ in range(ways // 2):
+        earlier.append(lax.ppermute(earlier[-1], "tensor", up))
+    for _ in range((ways - 1) // 2):
+        later.append(lax.ppermute(later[-1], "tensor", down))
+    line = jnp.concatenate([*earlier[::-1], *later[1:]], axis=1)
+    weighted_rows = jnp.roll(
+        line, (lax.axis_index("tensor") - ways // 2) * weighted.shape[1], axis=1
+    )
     cot_width = weighted_rows.shape[1]
     route_cot = (gate_values[:, :, None] * weighted_rows[:, None, :].astype(jnp.float32)).astype(
         jnp.bfloat16

time: 358 us -> 358 us (level); the launches traced: 357 us -> 352 us
  waiting for transfers between devices: 182 us -> 172 us
  starting transfers between devices: 19.2 us -> 26 us
    all_gather x1 -> x0, waiting for transfers between devices: 22.7 us -> none  [per_device(): weighted_rows = lax.all_gather(weighted, 'tensor', axis=1, tiled=True)]
    ppermute x0 -> x7, waiting for transfers between devices: none -> 19 us  [the longest x4 19 us: per_device(): earlier.append(lax.ppermute(earlier[-1], 'tensor', up))]
    ppermute x0 -> x7, starting transfers between devices: none -> 8.88 us  [the longest x3 8.87 us: per_device(): later.append(lax.ppermute(later[-1], 'tensor', down))]
    all_to_all x1, waiting for transfers between devices: 94.4 us -> 89.7 us  [per_device(): lax.all_to_all(send_cot, 'expert', split_axis=0, concat_axis=0, tiled=True)]
  transfers between devices with their start and end apart: 5 -> 11, of which waited for: 5 -> 8; matrix products, arithmetic and copies ran while one was open for 3% -> 4% of each run, Pallas kernels for 0% -> 0%
where the time goes in v1:
time: 358 us; the launch traced here: 352 us
  waiting for transfers between devices  172 us (48%)
  local copies, waits for them, and re-layouts  49.9 us (14%)
  matrix products  34.2 us (10%)
  blocking collectives  30.7 us (9%)
  starting transfers between devices  26 us (7%)
  other arithmetic  24.9 us (7%)
  between operations  14.4 us (4%)
    all_to_all x1, waiting for transfers between devices, per_device(): lax.all_to_all(send_cot, 'expert', split_axis=0, concat_axis=0, tiled=True)  89.7 us
    reduce_scatter x1, waiting for transfers between devices, per_device(): lax.psum_scatter(partial_value.astype(jnp.bfloat16), 'tensor', scatter_di...  40.1 us
    all_to_all x1, blocking collectives, per_device(): lax.all_to_all(send_inputs, 'expert', split_axis=0, concat_axis=0, tiled=...  30.7 us
    ppermute x4, waiting for transfers between devices, per_device(): earlier.append(lax.ppermute(earlier[-1], 'tensor', up))  19 us
    mul x3, local copies, waits for them, and re-layouts, per_device(): gate_values[:, :, None] * weighted_rows[:, None, :].astype(jnp.float32)  16.6 us
    scatter x1, local copies, waits for them, and re-layouts, per_device(): jnp.zeros((slots_total, 2, width), jnp.bfloat16).at[positions]  13.8 us
    all_to_all x1, waiting for transfers between devices, per_device(): lax.all_to_all(cross.reshape(experts, capacity, width), 'expert', split_a...  13.6 us
    scatter x1, other arithmetic, per_device(): send_cot = jnp.zeros((slots_total, cot_width), jnp.bfloat16).at[positions...  12.9 us
  transfers between devices with their start and end apart: 11, of which 8 were waited for; matrix products, arithmetic and copies ran while one was open for 4% of the time, Pallas kernels for 0%

profile of v1, /device:TPU:0, one launch (start us, length us, event | category | flops | bytes accessed | tf_op | source)
XLA Modules:
  0.0 351.8 jit_solution(1904513922638731330)
XLA Ops:
  7.2 0.0 reduce-scatter.2.cloned.1.call-start
  7.2 0.7 broadcast_multiply_fusion.1
  7.9 0.8 copy.32
  8.7 0.1 eq.32
  8.9 0.1 eq.28
  9.0 0.1 copy.31
  9.1 0.1 mul.99
  9.3 1.2 reduce-window.6
  10.5 0.2 slice_reduce_fusion
  10.7 0.1 fusion.9
  10.8 1.6 broadcast_in_dim.7
  12.4 0.8 broadcast_in_dim.6
  13.2 13.8 %scatter_fusion = bf16[768,2,512]{2,1,0:T(2,128)(2,1)S(1)} fusion(bf16[768,2,512]{2,1,0:T(2,128)(2,1)S(1)} %broadcast_in_dim.6, s32[512]{0:T(512)S(1)} %bitcast.61, bf16[512,2,512]{2,1,0:T(2,128)(2,1)S(1)} %bitcast.57), kind=kCustom, calls=%fused_computation.2 | custom fusion | bytes 3147776 | tf_op jit(solution)/shard_map/scatter | solution.py:28
  27.1 30.7 %all_to_all.20 = bf16[16,48,2,512]{3,2,1,0:T(2,128)(2,1)S(1)} all-to-all(bf16[16,48,2,512]{3,2,1,0:T(2,128)(2,1)S(1)} %bitcast.54), channel_id=1, replica_groups=mesh['expert'=16,'tensor'=8] {'expert'}, dimensions={0} | all-to-all | bytes 3145728 | tf_op jit(solution)/shard_map/all_to_all | solution.py:54
  57.8 0.4 copy.39
  58.2 0.0 copy-start.1
  58.2 1.2 copy-done.1
  59.5 11.9 %convolution_convert_fusion = bf16[768,4096]{1,0:T(8,128)(2,1)} fusion(bf16[768,1024]{1,0:T(8,128)(2,1)S(1)} %bitcast.59, bf16[1024,4096]{1,0:T(8,128)(2,1)} %bitcast.67), kind=kOutput, calls=%fused_computation.6 | convolution fusion | flops 6445596672 | bytes 16252928 | tf_op jit(solution)/shard_map/dot_general | solution.py:59
  71.4 0.0 reduce-scatter.2.cloned.1.call-update
  71.4 40.1 %reduce-scatter.2.cloned.1.call-done = bf16[768,512]{1,0:T(8,128)(2,1)} async-done(((bf16[768,4096]{1,0:T(8,128)(2,1)}), bf16[768,512]{1,0:T(8,128)(2,1)}) %reduce-scatter.2.cloned.1.call-update) | async-done | bytes 786448 | tf_op jit(solution)/shard_map/reduce_scatter | solution.py:60
  111.5 2.2 add_convert_fusion
  113.6 7.0 %all-to-all-start.1 = ((bf16[16,48,512]{2,1,0:T(8,128)(2,1)}), bf16[16,48,512]{2,1,0:T(8,128)(2,1)S(1)}, u32[]{:S(2)}, u32[]{:S(2)}) async-start(bf16[16,48,512]{2,1,0:T(8,128)(2,1)} %bitcast.7), calls=%async_computation.2 | async-start | bytes 1572864 | tf_op jit(solution)/shard_map/all_to_all | solution.py:64
  120.6 0.0 copy-start
  120.6 0.0 copy-start.2
  120.7 0.0 copy-start.3
  120.7 0.1 copy.30
  120.8 13.6 %all-to-all-done.1 = bf16[16,48,512]{2,1,0:T(8,128)(2,1)S(1)} async-done(((bf16[16,48,512]{2,1,0:T(8,128)(2,1)}), bf16[16,48,512]{2,1,0:T(8,128)(2,1)S(1)}, u32[]{:S(2)}, u32[]{:S(2)}) %all-to-all-start.1) | async-done | bytes 786464 | tf_op jit(solution)/shard_map/all_to_all | solution.py:64
  134.4 2.0 gather_fusion
  136.4 0.7 reshape.161
  137.1 1.3 multiply_reduce_fusion
  138.4 1.0 fusion.6
  139.4 0.0 collective-permute-start
  139.4 7.0 %collective-permute-done = bf16[256,512]{1,0:T(8,128)(2,1)S(1)} collective-permute-done((bf16[256,512]{1,0:T(8,128)(2,1)S(1)}, bf16[256,512]{1,0:T(8,128)(2,1)S(1)}, u32[]{:S(2)}, u32[]{:S(2)}) %collective-permute-start) | collective-permute-done | bytes 262176 | tf_op jit(solution)/shard_map/ppermute | solution.py:36
  146.4 0.0 collective-permute-start.1
  146.4 3.0 collective-permute-start.4
  149.4 4.1 %collective-permute-done.1 = bf16[256,512]{1,0:T(8,128)(2,1)S(1)} collective-permute-done((bf16[256,512]{1,0:T(8,128)(2,1)S(1)}, bf16[256,512]{1,0:T(8,128)(2,1)S(1)}, u32[]{:S(2)}, u32[]{:S(2)}) %collective-permute-start.1) | collective-permute-done | bytes 262176 | tf_op jit(solution)/shard_map/ppermute | solution.py:36
  153.5 0.0 collective-permute-start.2
  153.5 0.0 collective-permute-done.4
  153.5 3.0 collective-permute-start.5
  156.4 4.0 %collective-permute-done.2 = bf16[256,512]{1,0:T(8,128)(2,1)S(1)} collective-permute-done((bf16[256,512]{1,0:T(8,128)(2,1)S(1)}, bf16[256,512]{1,0:T(8,128)(2,1)S(1)}, u32[]{:S(2)}, u32[]{:S(2)}) %collective-permute-start.2) | collective-permute-done | bytes 262176 | tf_op jit(solution)/shard_map/ppermute | solution.py:36
  160.5 0.0 collective-permute-start.3
  160.5 0.1 mul.105
  160.6 0.0 collective-permute-done.5
  160.6 3.0 collective-permute-start.6
  163.6 3.9 %collective-permute-done.3 = bf16[256,512]{1,0:T(8,128)(2,1)S(1)} collective-permute-done((bf16[256,512]{1,0:T(8,128)(2,1)S(1)}, bf16[256,512]{1,0:T(8,128)(2,1)S(1)}, u32[]{:S(2)}, u32[]{:S(2)}) %collective-permute-start.3) | collective-permute-done | bytes 262176 | tf_op jit(solution)/shard_map/ppermute | solution.py:36
  167.7 0.0 collective-permute-done.6
  168.0 0.5 dynamic-slice_convert_fusion
  168.5 5.6 %mul.109 = f32[256,2,4096]{2,1,0:T(2,128)} broadcast(f32[256,4096]{1,0:T(8,128)S(1)} %dynamic-slice_convert_fusion), dimensions={0,2} | broadcast | bytes 12582912 | tf_op jit(solution)/shard_map/mul | solution.py:44
  174.2 10.9 %mul.110 = f32[512,4096]{1,0:T(8,128)} reshape(f32[256,2,4096]{2,1,0:T(2,128)} %mul.109) | data formatting | bytes 16777216 | tf_op jit(solution)/shard_map/mul | solution.py:44
  185.0 12.9 %scatter_custom_fusion.1 = bf16[768,4096]{1,0:T(8,128)(2,1)} fusion(s32[512]{0:T(512)S(1)} %bitcast.63, f32[512,4096]{1,0:T(8,128)} %mul.110, f32[512]{0:T(512)S(1)} %mul.105, bf16[]{:T(256)} %constant.64.clone.1), kind=kCustom, calls=%fused_computation.7 | custom fusion | flops 4194304 | bytes 14682114 | tf_op jit(solution)/shard_map/scatter | solution.py:50
  198.0 4.6 %all-to-all-start.2 = ((bf16[16,48,4096]{2,1,0:T(8,128)(2,1)}), bf16[16,48,4096]{2,1,0:T(8,128)(2,1)}, u32[]{:S(2)}, u32[]{:S(2)}) async-start(bf16[16,48,4096]{2,1,0:T(8,128)(2,1)} %bitcast.53), calls=%async_computation.3 | async-start | bytes 12582912 | tf_op jit(solution)/shard_map/all_to_all | solution.py:55
  202.6 89.7 %all-to-all-done.2 = bf16[16,48,4096]{2,1,0:T(8,128)(2,1)} async-done(((bf16[16,48,4096]{2,1,0:T(8,128)(2,1)}), bf16[16,48,4096]{2,1,0:T(8,128)(2,1)}, u32[]{:S(2)}, u32[]{:S(2)}) %all-to-all-start.2) | async-done | bytes 6291488 | tf_op jit(solution)/shard_map/all_to_all | solution.py:55
  292.3 11.0 %convolution_convert_fusion.1 = bf16[768,1024]{1,0:T(8,128)(2,1)S(1)} fusion(bf16[768,4096]{1,0:T(8,128)(2,1)} %bitcast.11, bf16[1024,4096]{1,0:T(8,128)(2,1)} %bitcast.68), kind=kOutput, calls=%fused_computation.12 | convolution fusion | flops 6443237376 | bytes 16252928 | tf_op jit(solution)/shard_map/dot_general | solution.py:81
  303.3 1.3 convert_reduce_fusion.1
  304.6 2.4 reshape.157
  307.0 5.4 %all-to-all-start.3 = ((bf16[16,48,2,512]{3,2,1,0:T(2,128)(2,1)}), bf16[16,48,2,512]{3,2,1,0:T(2,128)(2,1)S(1)}, u32[]{:S(2)}, u32[]{:S(2)}) async-start(bf16[16,48,2,512]{3,2,1,0:T(2,128)(2,1)} %reshape.157), calls=%async_computation.4 | async-start | bytes 3145728 | tf_op jit(solution)/shard_map/all_to_all | solution.py:88
  312.4 0.6 broadcast_multiply_fusion
  313.0 11.4 %multiply_convert_fusion = bf16[1024,4096]{1,0:T(8,128)(2,1)} fusion(bf16[768,1024]{1,0:T(8,128)(2,1)} %bitcast.60, bf16[768,4096]{1,0:T(8,128)(2,1)} %bitcast.11), kind=kOutput, calls=%fused_computation.4 | convolution fusion | flops 6450839552 | bytes 16252928 | tf_op jit(solution)/shard_map/dot_general | solution.py:78
  324.3 9.2 %all-to-all-done.3 = bf16[16,48,2,512]{3,2,1,0:T(2,128)(2,1)S(1)} async-done(((bf16[16,48,2,512]{3,2,1,0:T(2,128)(2,1)}), bf16[16,48,2,512]{3,2,1,0:T(2,128)(2,1)S(1)}, u32[]{:S(2)}, u32[]{:S(2)}) %all-to-all-start.3) | async-done | bytes 1572896 | tf_op jit(solution)/shard_map/all_to_all | solution.py:88
  333.5 3.6 %gather_fusion.1 = bf16[512,2,512]{2,1,0:T(2,128)(2,1)S(1)} fusion(bf16[768,2,512]{2,1,0:T(2,128)(2,1)S(1)} %bitcast.56, s32[1024]{0:T(1024)S(1)} %pad_clamp_fusion), kind=kCustom, calls=%fused_computation.1 | custom fusion | bytes 2099200 | tf_op jit(solution)/shard_map/gather | solution.py:96
  337.1 1.4 convert_reduce_fusion
  338.6 0.5 slice_add_fusion
  339.1 4.7 %scatter-add.4 = f32[256,2,512]{2,1,0:T(2,128)S(1)} dynamic-update-slice(f32[256,2,512]{2,1,0:T(2,128)S(1)} %convert_reduce_fusion, f32[256,1,512]{2,1,0:T(1,128)S(1)} %slice_add_fusion, s32[]{:T(128)} %constant.66.clone.1, s32[]{:T(128)} %constant.66.clone.1, s32[]{:T(128)} %constant.66.clone.1) | dynamic-update-slice | bytes 1048580 | tf_op jit(solution)/shard_map/scatter-add | solution.py:101
  343.8 1.2 convert_element_type.90
  (29 shorter events, 0.5 us)
Async XLA Ops:
  7.2 104.3 %reduce-scatter.2.cloned.1.call-start = ((), (), s32[]{:S(2)}) async-start(), calls=%async_computation.5 | async-start | bytes 7077888 | tf_op jit(solution)/shard_map/reduce_scatter | solution.py:60
  58.2 1.2 copy-start.1
  71.4 40.1 %copy-start.5 = (f32[1,512]{1,0:T(1,128)S(1)}, f32[1,512]{1,0:T(1,128)}, u32[]{:S(2)}) copy-start(f32[1,512]{1,0:T(1,128)} %param.13) | copy-start | bytes 6148
  71.4 49.3 %copy-start.4 = (f32[256,2]{0,1:T(2,128)S(1)}, f32[256,2]{0,1:T(2,128)}, u32[]{:S(2)}) copy-start(f32[256,2]{0,1:T(2,128)} %param.15) | copy-start | bytes 6148
  113.6 20.8 %all-to-all-start.1 = ((bf16[16,48,512]{2,1,0:T(8,128)(2,1)}), bf16[16,48,512]{2,1,0:T(8,128)(2,1)S(1)}, u32[]{:S(2)}, u32[]{:S(2)}) async-start(bf16[16,48,512]{2,1,0:T(8,128)(2,1)} %bitcast.7), calls=%async_computation.2 | async-start | bytes 1572864 | tf_op jit(solution)/shard_map/all_to_all | solution.py:64
  120.6 17.8 %copy-start = (bf16[256,2,512]{2,1,0:T(2,128)(2,1)S(1)}, bf16[256,2,512]{2,1,0:T(2,128)(2,1)}, u32[]{:S(2)}) copy-start(bf16[256,2,512]{2,1,0:T(2,128)(2,1)} %param.9) | copy-start | bytes 1572868
  120.6 17.8 %copy-start.2 = (bf16[256,512]{1,0:T(8,128)(2,1)S(1)}, bf16[256,512]{1,0:T(8,128)(2,1)}, u32[]{:S(2)}) copy-start(bf16[256,512]{1,0:T(8,128)(2,1)} %param.11) | copy-start | bytes 786436
  120.7 17.8 %copy-start.3 = (bf16[256,512]{1,0:T(8,128)(2,1)S(1)}, bf16[256,512]{1,0:T(8,128)(2,1)}, u32[]{:S(2)}) copy-start(bf16[256,512]{1,0:T(8,128)(2,1)} %param.10) | copy-start | bytes 786436
  139.4 7.0 %collective-permute-start = (bf16[256,512]{1,0:T(8,128)(2,1)S(1)}, bf16[256,512]{1,0:T(8,128)(2,1)S(1)}, u32[]{:S(2)}, u32[]{:S(2)}) collective-permute-start(bf16[256,512]{1,0:T(8,128)(2,1)S(1)} %get-tuple-element.29), channel_id=1, source_target_pairs={{0,1},{1,2},{2,3},{3,4},{4,5},{5,6},{6,7},{7,0},{8,9},{9,10},{10,1... | collective-permute-start | bytes 786440 | tf_op jit(solution)/shard_map/ppermute | solution.py:36
  146.4 7.0 %collective-permute-start.1 = (bf16[256,512]{1,0:T(8,128)(2,1)S(1)}, bf16[256,512]{1,0:T(8,128)(2,1)S(1)}, u32[]{:S(2)}, u32[]{:S(2)}) collective-permute-start(bf16[256,512]{1,0:T(8,128)(2,1)S(1)} %collective-permute-done), channel_id=1, source_target_pairs={{0,1},{1,2},{2,3},{3,4},{4,5},{5,6},{6,7},{7,0},{8,9},{9,10},{10,1... | collective-permute-start | bytes 786440 | tf_op jit(solution)/shard_map/ppermute | solution.py:36
  146.4 7.0 %collective-permute-start.4 = (bf16[256,512]{1,0:T(8,128)(2,1)S(1)}, bf16[256,512]{1,0:T(8,128)(2,1)S(1)}, u32[]{:S(2)}, u32[]{:S(2)}) collective-permute-start(bf16[256,512]{1,0:T(8,128)(2,1)S(1)} %get-tuple-element.29), channel_id=1, source_target_pairs={{0,7},{1,0},{2,1},{3,2},{4,3},{5,4},{6,5},{7,6},{8,15},{9,8},{10,9... | collective-permute-start | bytes 786440 | tf_op jit(solution)/shard_map/ppermute | solution.py:38
  153.5 7.0 %collective-permute-start.2 = (bf16[256,512]{1,0:T(8,128)(2,1)S(1)}, bf16[256,512]{1,0:T(8,128)(2,1)S(1)}, u32[]{:S(2)}, u32[]{:S(2)}) collective-permute-start(bf16[256,512]{1,0:T(8,128)(2,1)S(1)} %collective-permute-done.1), channel_id=1, source_target_pairs={{0,1},{1,2},{2,3},{3,4},{4,5},{5,6},{6,7},{7,0},{8,9},{9,10},{10,1... | collective-permute-start | bytes 786440 | tf_op jit(solution)/shard_map/ppermute | solution.py:36
  153.5 7.2 %collective-permute-start.5 = (bf16[256,512]{1,0:T(8,128)(2,1)S(1)}, bf16[256,512]{1,0:T(8,128)(2,1)S(1)}, u32[]{:S(2)}, u32[]{:S(2)}) collective-permute-start(bf16[256,512]{1,0:T(8,128)(2,1)S(1)} %collective-permute-done.4), channel_id=1, source_target_pairs={{0,7},{1,0},{2,1},{3,2},{4,3},{5,4},{6,5},{7,6},{8,15},{9,8},{10,9... | collective-permute-start | bytes 786440 | tf_op jit(solution)/shard_map/ppermute | solution.py:38
  160.5 7.0 %collective-permute-start.3 = (bf16[256,512]{1,0:T(8,128)(2,1)S(1)}, bf16[256,512]{1,0:T(8,128)(2,1)S(1)}, u32[]{:S(2)}, u32[]{:S(2)}) collective-permute-start(bf16[256,512]{1,0:T(8,128)(2,1)S(1)} %collective-permute-done.2), channel_id=1, source_target_pairs={{0,1},{1,2},{2,3},{3,4},{4,5},{5,6},{6,7},{7,0},{8,9},{9,10},{10,1... | collective-permute-start | bytes 786440 | tf_op jit(solution)/shard_map/ppermute | solution.py:36
  160.6 7.1 %collective-permute-start.6 = (bf16[256,512]{1,0:T(8,128)(2,1)S(1)}, bf16[256,512]{1,0:T(8,128)(2,1)S(1)}, u32[]{:S(2)}, u32[]{:S(2)}) collective-permute-start(bf16[256,512]{1,0:T(8,128)(2,1)S(1)} %collective-permute-done.5), channel_id=1, source_target_pairs={{0,7},{1,0},{2,1},{3,2},{4,3},{5,4},{6,5},{7,6},{8,15},{9,8},{10,9... | collective-permute-start | bytes 786440 | tf_op jit(solution)/shard_map/ppermute | solution.py:38
  198.0 94.3 %all-to-all-start.2 = ((bf16[16,48,4096]{2,1,0:T(8,128)(2,1)}), bf16[16,48,4096]{2,1,0:T(8,128)(2,1)}, u32[]{:S(2)}, u32[]{:S(2)}) async-start(bf16[16,48,4096]{2,1,0:T(8,128)(2,1)} %bitcast.53), calls=%async_computation.3 | async-start | bytes 12582912 | tf_op jit(solution)/shard_map/all_to_all | solution.py:55
  307.0 26.6 %all-to-all-start.3 = ((bf16[16,48,2,512]{3,2,1,0:T(2,128)(2,1)}), bf16[16,48,2,512]{3,2,1,0:T(2,128)(2,1)S(1)}, u32[]{:S(2)}, u32[]{:S(2)}) async-start(bf16[16,48,2,512]{3,2,1,0:T(2,128)(2,1)} %reshape.157), calls=%async_computation.4 | async-start | bytes 3145728 | tf_op jit(solution)/shard_map/all_to_all | solution.py:88
Sparse Core Ops, SparseCore 0:
  71.5 39.9 reduce-scatter.1
